TPU v7x, 32 devices: a whole 2x2x4 slice. The times are simulated.
32 devices in a mesh: groups: 2 (over y), outer: 2 (over core), inner: 8 (over z, x).
Axes of the slice: x: 2, y: 2, z: 4, core: 2. Of those that a mesh axis runs over, the one named last changes fastest.
Arguments:
- leftover_inputs: bfloat16 [240, 8192], P('groups', ('outer', 'inner')), parts along dimension 0, may hold values from -6 to 6
- codebook_matrix: bfloat16 [8192, 8192], P(('groups', 'outer', 'inner')), parts along dimension 0, may hold values from -0.198873782 to 0.198873782
- remaining_tiles: int32 [32, 2], P(('groups', 'outer', 'inner')), parts along dimension 0, may hold values from 0 to 1, as said below
Outputs:
- screen: float32 [240, 4096], P('groups', ('outer', 'inner')), parts along dimension 0
- coefficients: float32 [240, 4096], P('groups', ('outer', 'inner')), parts along dimension 0
- residual: float32 [240, 8192], P('groups', ('outer', 'inner')), parts along dimension 0
There are 2 independent parts, one for each index of `groups`. A program takes and returns all parts, laid end to end along the dimension named above; each array names one. Nothing has to cross between parts.
Inputs may be any that keep to these rules, and one draw needn't show every extreme that they name: `remaining_tiles`: in every run of 8 devices along inner (one outer index), exactly 2 devices have both blocks surviving and 1 have one.
All inputs are finite; a program needn't handle non-finite values. Where the computation divides by a largest or mean magnitude, that divisor is 1e-20 or more.
Results may differ from a plain program's by a relative error of at most 0.0019.
Values may be sent and summed in bfloat16 or wider, within the bound.
A program may use at most 128 MiB of HBM per device.

v0:
```python
import math

import jax
import jax.numpy as jnp
from jax import lax
from jax.sharding import PartitionSpec as P

GROUP_ELEMENTS = 128
BLK_DEV = 2


penalty_ratio = 0.1
epsilon = 1e-06


def shrink(values, threshold):
    return values - jnp.clip(values, -threshold, threshold)


def on_device(leftover_inputs, codebook_matrix, remaining_tiles):
    shard_count = lax.axis_size(("outer", "inner"))
    atoms_local, width = codebook_matrix.shape
    tokens, slab_width = leftover_inputs.shape
    atoms_total = atoms_local * shard_count
    shard_piece = lax.all_gather(leftover_inputs, ("outer", "inner"), axis=1, tiled=True)
    correlation = lax.dot_general(
        shard_piece, codebook_matrix, (((1,), (1,)), ((), ())), preferred_element_type=jnp.float32
    )
    widened = shard_piece.astype(jnp.float32)
    energy = jnp.sum(widened * widened, axis=1)
    whole_signals = shard_piece
    correlation, energy, whole_signals = (correlation, energy, whole_signals)
    atom_squares = jnp.sum(jnp.square(codebook_matrix.astype(jnp.float32)), axis=1)
    local_peak = jnp.max(jnp.abs(correlation), axis=1)
    peak_value, widest = lax.pmax((local_peak, jnp.max(atom_squares)), ("outer", "inner"))
    peak_value = peak_value + epsilon
    lipschitz = (1.0 + math.sqrt(atoms_total / width)) ** 2 * (widest + epsilon)
    atom_norm = jnp.sqrt(atom_squares + epsilon)
    radius = (1.0 / penalty_ratio - 1.0) * jnp.sqrt(energy + epsilon)
    screen = (jnp.abs(correlation) + radius[:, None] * atom_norm[None, :]) / peak_value[:, None]
    threshold = (penalty_ratio * peak_value / lipschitz)[:, None]
    block_rows = codebook_matrix.reshape(BLK_DEV, GROUP_ELEMENTS, width)
    block_corr = correlation.reshape(tokens, BLK_DEV, GROUP_ELEMENTS)
    retained_element_indicators = remaining_tiles[0]
    work_rows = [block_rows[slot_index] for slot_index in range(BLK_DEV)]
    work_corr = [block_corr[:, slot_index] for slot_index in range(BLK_DEV)]
    work_flags = [retained_element_indicators[slot_index] for slot_index in range(BLK_DEV)]

    def first_of(corr_part, keep_flag_value):
        return keep_flag_value.astype(jnp.float32) * shrink(corr_part / lipschitz, threshold)

    def rebuild(first_part, row_portion, keep_flag_value):
        return lax.cond(
            keep_flag_value > 0,
            lambda: jnp.dot(
                first_part.astype(jnp.bfloat16), row_portion, preferred_element_type=jnp.float32
            ),
            lambda: jnp.zeros((tokens, width), jnp.float32),
        )

    first_parts = [
        first_of(work_corr[slot_index], work_flags[slot_index]) for slot_index in range(BLK_DEV)
    ]
    partial_term = rebuild(first_parts[0], work_rows[0], work_flags[0])
    slot_index = 1
    partial_term = partial_term + rebuild(
        first_parts[slot_index], work_rows[slot_index], work_flags[slot_index]
    )
    slab_sum = lax.psum_scatter(partial_term, ("outer", "inner"), scatter_dimension=1, tiled=True)
    residual = slab_sum - leftover_inputs.astype(jnp.float32)
    residual_half = lax.all_gather(
        residual.astype(jnp.bfloat16), ("outer", "inner"), axis=1, tiled=True
    )

    def refine(first_part, row_portion, keep_flag_value):

        def active():
            gradient = lax.dot_general(
                residual_half,
                row_portion,
                (((1,), (1,)), ((), ())),
                preferred_element_type=jnp.float32,
            )
            return keep_flag_value.astype(jnp.float32) * shrink(
                first_part - gradient / lipschitz, threshold
            )

        return lax.cond(
            keep_flag_value > 0, active, lambda: jnp.zeros((tokens, GROUP_ELEMENTS), jnp.float32)
        )

    second_parts = [
        refine(first_parts[slot_index], work_rows[slot_index], work_flags[slot_index])
        for slot_index in range(BLK_DEV)
    ]
    coefficients = jnp.concatenate(second_parts, axis=1)
    return (screen, coefficients, residual)


def solution(mesh):
    in_specs = (
        P("groups", ("outer", "inner")),
        P(("groups", "outer", "inner"), None),
        P(("groups", "outer", "inner"), None),
    )
    out_specs = (
        P("groups", ("outer", "inner")),
        P("groups", ("outer", "inner")),
        P("groups", ("outer", "inner")),
    )
    return jax.shard_map(
        on_device, mesh=mesh, in_specs=in_specs, out_specs=out_specs, check_vma=False
    )
```

profile of v0, /device:TPU:8, one launch (start us, length us, event | category | flops | bytes accessed | tf_op | source)
XLA Modules:
  0.0 224.5 jit_solution(1478570167703303798)
XLA Ops:
  7.2 0.0 all-gather.3.cloned.1.call-start
  7.2 0.7 all-gather.3.cloned.1.call-update
  7.9 0.0 reduce-scatter.2.cloned.1.call-start
  7.9 1.4 fusion.14
  12.1 0.0 copy-start
  12.1 3.3 %multiply_reduce_fusion = f32[256]{0:T(256)S(1)} fusion(bf16[256,8192]{1,0:T(8,128)(2,1)} %param.12), kind=kLoop, calls=%fused_computation.12 | loop fusion | flops 6291200 | bytes 4195328 | tf_op jit(solution)/shard_map/reduce_sum | solution.py:33
  15.3 0.6 add_sqrt_fusion
  15.9 1.9 fusion.12
  17.8 33.5 %all-gather.3.cloned.1.call-done = bf16[120,8192]{1,0:T(8,128)(2,1)} async-done(((bf16[120,512]{1,0:T(8,128)(2,1)}), bf16[120,8192]{1,0:T(8,128)(2,1)}) %all-gather.3.cloned.1.call-update) | async-done | bytes 1966096 | tf_op jit(solution)/shard_map/all_gather | solution.py:25
  51.4 4.4 %abs_reduce_fusion = (f32[120]{0:T(128)S(1)}, f32[120,256]{1,0:T(8,128)S(1)}) fusion(bf16[120,8192]{1,0:T(8,128)(2,1)} %all-gather.3.cloned.1.call-done, bf16[256,8192]{1,0:T(8,128)(2,1)} %param.12), kind=kOutput, calls=%fused_computation.17 | convolution fusion | flops 503377792 | bytes 6283744 | tf_op jit(solution)/shard_map/dot_general | solution.py:26
  55.7 0.1 reshape.35
  55.8 0.1 fusion.13
  55.9 31.2 %all-reduce = (f32[120]{0:T(128)S(1)}, f32[]{:T(128)}) all-reduce(f32[120]{0:T(128)S(1)} %get-tuple-element.80, f32[]{:T(128)} %get-tuple-element.76), channel_id=1, replica_groups=mesh['groups'=2,'outer'=2,'inner'=8] {'outer','inner'}, use_global_device_ids=true, to_apply=%region_3.0 | all-reduce | flops 121 | bytes 968 | tf_op jit(solution)/shard_map/pmax | solution.py:35
  87.8 0.1 fusion.7
  87.9 2.6 %conditional.4 = (f32[120,8192]{1,0:T(8,128)}) conditional(s32[]{:T(128)} %convert_element_type.40, () %tuple.33, (f32[120,128]{1,0:T(8,128)S(1)}, bf16[128,8192]{1,0:T(8,128)(2,1)S(1)}) %tuple.34), branch_computations={%region_6.7_spmd, %region_7.8_spmd} | conditional | flops 251673600 | bytes 6090760 | solution.py:53
  87.9 2.6 %fusion = f32[120,8192]{1,0:T(8,128)} fusion(bf16[128,8192]{1,0:T(8,128)(2,1)S(1)} %get-tuple-element.38, f32[120,128]{1,0:T(8,128)S(1)} %get-tuple-element.37), kind=kOutput, calls=%fused_computation | convolution fusion | flops 251673600 | bytes 6090752 | tf_op jit(solution)/shard_map/cond/branch_1_fun/dot_general | solution.py:55
  90.5 4.2 %conditional.5 = (f32[120,8192]{1,0:T(8,128)}) conditional(s32[]{:T(128)} %convert_element_type.42, () %tuple.35, (f32[120,128]{1,0:T(8,128)S(1)}, bf16[128,8192]{1,0:T(8,128)(2,1)}) %tuple.36), branch_computations={%region_8.9_spmd, %region_9.10_spmd} | conditional | flops 251673600 | bytes 6090760 | solution.py:53
  90.5 4.2 %fusion.2 = f32[120,8192]{1,0:T(8,128)} fusion(bf16[128,8192]{1,0:T(8,128)(2,1)} %get-tuple-element.40, f32[120,128]{1,0:T(8,128)S(1)} %get-tuple-element.39), kind=kOutput, calls=%fused_computation.2 | convolution fusion | flops 251673600 | bytes 6090752 | tf_op jit(solution)/shard_map/cond/branch_1_fun/dot_general | solution.py:55
  94.7 5.6 %add.37 = f32[120,8192]{1,0:T(8,128)} add(f32[120,8192]{1,0:T(8,128)} %get-tuple-element.82, f32[120,8192]{1,0:T(8,128)} %get-tuple-element.83) | non-fusion elementwise | flops 983040 | bytes 11796480 | tf_op jit(solution)/shard_map/add | solution.py:66
  100.3 0.0 reduce-scatter.2.cloned.1.call-update
  100.4 0.0 all-gather.5.cloned.1.call-start
  100.4 67.8 %reduce-scatter.2.cloned.1.call-done = f32[120,512]{1,0:T(8,128)} async-done(((f32[120,8192]{1,0:T(8,128)}), f32[120,512]{1,0:T(8,128)}) %reduce-scatter.2.cloned.1.call-update) | async-done | bytes 245776 | tf_op jit(solution)/shard_map/reduce_scatter | solution.py:69
  168.2 1.7 fusion.10
  169.9 0.0 all-gather.5.cloned.1.call-update
  169.9 2.0 multiply_reduce_fusion.1
  172.0 0.8 add_divide_fusion
  172.7 38.0 %all-gather.5.cloned.1.call-done = bf16[120,8192]{1,0:T(8,128)(2,1)} async-done(((bf16[120,512]{1,0:T(8,128)(2,1)}), bf16[120,8192]{1,0:T(8,128)(2,1)}) %all-gather.5.cloned.1.call-update) | async-done | bytes 1966096 | tf_op jit(solution)/shard_map/all_gather | solution.py:71
  210.7 3.6 %conditional.7 = (f32[120,128]{1,0:T(8,128)S(1)}) conditional(s32[]{:T(128)} %convert_element_type.42, () %tuple.38, (s32[]{:T(128)}, bf16[120,8192]{1,0:T(8,128)(2,1)}, bf16[128,8192]{1,0:T(8,128)(2,1)}, f32[]{:T(128)}, f32[120,128]{1,0:T(8,128)S(1)}, /*index=5*/f32[120,1]{0,1:T(1,128)S(1)}) %tuple.64), branch_computations={%region_13.14_spmd, %region_14.15_spmd} | conditional | flops 251750528 | bytes 4188056 | solution.py:88
  211.5 2.9 %subtract_multiply_fusion.1 = f32[120,128]{1,0:T(8,128)S(1)} fusion(f32[120,128]{1,0:T(8,128)S(1)} %get-tuple-element.55, bf16[120,8192]{1,0:T(8,128)(2,1)} %get-tuple-element.56, bf16[128,8192]{1,0:T(8,128)(2,1)} %get-tuple-element.57, f32[120]{0:T(128)S(1)} %negate_bitcast_fusion.1, f32[120]{0:T(128)S(1)} %bitcast.41, f32[]{:T(128)} %get-tuple-element.58, ...), kind=kOutput, calls=%fused_computation.10 | convolution fusion | flops 251750400 | bytes 4187080 | tf_op jit(solution)/shard_map/cond/branch_1_fun/dot_general | solution.py:78
  214.4 3.0 %conditional.6 = (f32[120,128]{1,0:T(8,128)S(1)}) conditional(s32[]{:T(128)} %convert_element_type.40, () %tuple.32, (s32[]{:T(128)}, bf16[120,8192]{1,0:T(8,128)(2,1)}, bf16[128,8192]{1,0:T(8,128)(2,1)S(1)}, f32[]{:T(128)}, f32[120,128]{1,0:T(8,128)S(1)}, /*index=5*/f32[120,1]{0,1:T(1,128)S(1)}) %tuple.65), branch_computations={%region_11.12_spmd, %region_12.13_spmd} | conditional | flops 251750528 | bytes 4188056 | solution.py:88
  215.1 2.3 %subtract_multiply_fusion = f32[120,128]{1,0:T(8,128)S(1)} fusion(f32[120,128]{1,0:T(8,128)S(1)} %get-tuple-element.49, bf16[120,8192]{1,0:T(8,128)(2,1)} %get-tuple-element.50, bf16[128,8192]{1,0:T(8,128)(2,1)S(1)} %get-tuple-element.51, f32[120]{0:T(128)S(1)} %negate_bitcast_fusion, f32[120]{0:T(128)S(1)} %bitcast.42, f32[]{:T(128)} %get-tuple-element.52, ...), kind=kOutput, calls=%fused_computation.6 | convolution fusion | flops 251750400 | bytes 4187080 | tf_op jit(solution)/shard_map/cond/branch_1_fun/dot_general | solution.py:78
  217.4 0.7 pad_maximum_fusion
  (7 shorter events, 0.0 us)
Async XLA Ops:
  7.2 44.2 %all-gather.3.cloned.1.call-start = ((), (), s32[]{:S(2)}) async-start(), calls=%async_computation.1 | async-start | bytes 2088960 | tf_op jit(solution)/shard_map/all_gather | solution.py:25
  7.9 160.3 %reduce-scatter.2.cloned.1.call-start = ((), (), s32[]{:S(2)}) async-start(), calls=%async_computation.2 | async-start | bytes 4177920 | tf_op jit(solution)/shard_map/reduce_scatter | solution.py:69
  12.1 3.9 %copy-start = (bf16[256,8192]{1,0:T(8,128)(2,1)S(1)}, bf16[256,8192]{1,0:T(8,128)(2,1)}, u32[]{:S(2)}) copy-start(bf16[256,8192]{1,0:T(8,128)(2,1)} %param.12) | copy-start | bytes 12582916
  100.3 67.8 %copy-start.1 = (bf16[120,512]{1,0:T(8,128)(2,1)S(1)}, bf16[120,512]{1,0:T(8,128)(2,1)}, u32[]{:S(2)}) copy-start(bf16[120,512]{1,0:T(8,128)(2,1)} %param.11) | copy-start | bytes 368644
  100.4 110.4 %all-gather.5.cloned.1.call-start = ((), (), s32[]{:S(2)}) async-start(), calls=%async_computation.3 | async-start | bytes 2088960 | tf_op jit(solution)/shard_map/all_gather | solution.py:71
Sparse Core Ops, SparseCore 0:
  10.1 41.2 all-gather.2
  100.5 67.6 reduce-scatter.1
  171.0 39.6 all-gather.4
where the time goes:
time: 226 us; the launch traced here: 225 us
  waiting for transfers between devices  140 us (62%)
  blocking collectives  31.2 us (14%)
  between operations  17.2 us (8%)
  matrix products  16.4 us (7%)
  other arithmetic  14.8 us (7%)
  local copies, waits for them, and re-layouts  3.44 us (2%)
    reduce_scatter x1, waiting for transfers between devices, on_device(): lax.psum_scatter(partial_term, ('outer', 'inner'), scatter_dimension=1, t...  67.8 us
    all_gather x1, waiting for transfers between devices, on_device(): lax.all_gather(residual.astype(jnp.bfloat16), ('outer', 'inner'), axis=1,...  38 us
    all_gather x1, waiting for transfers between devices, on_device(): lax.all_gather(leftover_inputs, ('outer', 'inner'), axis=1, tiled=True)  33.5 us
    pmax x1, blocking collectives, on_device(): lax.pmax((local_peak, jnp.max(atom_squares)), ('outer', 'inner'))  31.2 us
    dot_general x2, matrix products, rebuild(): jnp.dot(first_part.astype(jnp.bfloat16), row_portion, preferred_element_t...  6.78 us
    add x1, other arithmetic, on_device(): partial_term + rebuild(first_parts[slot_index], work_rows[slot_index], wo...  5.64 us
    dot_general x2, matrix products, active(): lax.dot_general(residual_half, row_portion, (((1,), (1,)), ((), ())), pre...  5.19 us
  transfers between devices with their start and end apart: 3, of which 3 were waited for; matrix products, arithmetic and copies ran while one was open for 4% of the time, Pallas kernels for 0%

commit v1 on v0

--- a/solution.py
+++ b/solution.py
@@ -1,8 +1,11 @@
+import functools
 import math
 
 import jax
 import jax.numpy as jnp
 from jax import lax
+from jax.experimental import pallas as pl
+from jax.experimental.pallas import tpu as pltpu
 from jax.sharding import PartitionSpec as P
 
 GROUP_ELEMENTS = 128
@@ -17,7 +20,7 @@
     return values - jnp.clip(values, -threshold, threshold)
 
 
-def on_device(leftover_inputs, codebook_matrix, remaining_tiles):
+def on_device_narrow(leftover_inputs, codebook_matrix, remaining_tiles):
     shard_count = lax.axis_size(("outer", "inner"))
     atoms_local, width = codebook_matrix.shape
     tokens, slab_width = leftover_inputs.shape
@@ -97,6 +100,366 @@
     return (screen, coefficients, residual)
 
 
+PIECES = 2
+LANES = 128
+
+
+def fused_kernel(
+    ring, width, step_scale,
+    x_ref, d_hbm, flags_ref,
+    screen_ref, coef_ref, resid_ref,
+    d_ref, x_all, r_all, peaks, sib_out, sib_in, right_out, right_in, left_out, left_in,
+    load_sem, ag1_send, ag1_recv, ag2_send, ag2_recv,
+    peak_send, peak_recv, sib_send, sib_recv, rs_send, rs_recv,
+):
+    tokens, slab = x_ref.shape
+    piece = slab // PIECES
+    shards = 2 * ring
+    right_hops, left_hops = ring // 2, ring // 2 - 1
+    core = lax.axis_index("outer")
+    chip = lax.axis_index("inner")
+    me = core * ring + chip
+    other = 1 - core
+
+    load = pltpu.make_async_copy(d_hbm, d_ref, load_sem)
+    load.start()
+
+    barrier = pltpu.get_barrier_semaphore()
+
+    def peer_of(offset):
+        peer = lax.rem(me + offset, shards)
+        return {"outer": lax.div(peer, ring), "inner": lax.rem(peer, ring)}
+
+    def greet(offset, carry):
+        pl.semaphore_signal(
+            barrier, inc=1, device_id=peer_of(offset), device_id_type=pl.DeviceIdType.MESH
+        )
+        return carry
+
+    lax.fori_loop(1, shards, greet, 0)
+
+    place = jnp.where(lax.rem(chip, 2) == 0, lax.div(chip, 2), ring - 1 - lax.div(chip, 2))
+
+    def chip_at(offset):
+        spot = lax.rem(place + offset + ring, ring)
+        return jnp.where(spot < ring // 2, 2 * spot, 2 * (ring - 1 - spot) + 1)
+
+    to_right = {"outer": core, "inner": chip_at(1)}
+    to_left = {"outer": core, "inner": chip_at(-1)}
+    to_sibling = {"outer": other, "inner": chip}
+
+    def remote(src, dst, send_sem, recv_sem, target):
+        return pltpu.make_async_remote_copy(
+            src_ref=src, dst_ref=dst, send_sem=send_sem, recv_sem=recv_sem,
+            device_id=target, device_id_type=pl.DeviceIdType.MESH,
+        )
+
+    def columns(chunk):
+        return d_ref[:, pl.ds(pl.multiple_of(chunk * piece, piece), piece)]
+
+    sent = []
+
+    class Gather:
+        def __init__(self, buf, send, recv):
+            self.buf, self.send, self.recv = buf, send, recv
+
+        def copy(self, row, part, chunk, target):
+            at = self.buf.at[chunk]
+            return remote(at, at, self.send.at[row, part], self.recv.at[row, part], target)
+
+        def start(self, row, part, chunk, target):
+            made = self.copy(row, part, chunk, target)
+            made.start()
+            sent.append(made)
+
+        def share(self, slot, part, chunk):
+            self.start(right_hops + left_hops + slot, part, chunk, to_sibling)
+
+        def chunk(self, side, offset, part):
+            return (side * ring + chip_at(offset)) * PIECES + part
+
+        def begin(self, part):
+            mine = self.chunk(core, 0, part)
+            self.start(0, part, mine, to_right)
+            self.start(right_hops, part, mine, to_left)
+            self.share(0, part, mine)
+
+        def run(self, consume):
+            for part in range(PIECES):
+                consume(self.chunk(core, 0, part))
+            shared = [(0, 0)]
+            for hop in range(right_hops):
+                fresh = []
+                for part in range(PIECES):
+                    got = self.chunk(core, -1 - hop, part)
+                    self.copy(hop, part, got, to_right).wait_recv()
+                    if hop + 1 < right_hops:
+                        self.start(hop + 1, part, got, to_right)
+                    self.share(1 + 2 * hop, part, got)
+                    if hop < left_hops:
+                        back = self.chunk(core, 1 + hop, part)
+                        self.copy(right_hops + hop, part, back, to_left).wait_recv()
+                        if hop + 1 < left_hops:
+                            self.start(right_hops + hop + 1, part, back, to_left)
+                        self.share(2 + 2 * hop, part, back)
+                        consume(back)
+                    consume(got)
+                fresh.append((1 + 2 * hop, -1 - hop))
+                if hop < left_hops:
+                    fresh.append((2 + 2 * hop, 1 + hop))
+                self.take(shared, consume)
+                shared = fresh
+            self.take(shared, consume)
+
+        def take(self, shared, consume):
+            for slot, offset in shared:
+                for part in range(PIECES):
+                    got = self.chunk(other, offset, part)
+                    self.copy(right_hops + left_hops + slot, part, got, to_sibling).wait_recv()
+                    consume(got)
+
+    first_gather = Gather(x_all, ag1_send, ag1_recv)
+    for part in range(PIECES):
+        x_all[me * PIECES + part] = x_ref[:, part * piece:(part + 1) * piece]
+    pl.semaphore_wait(barrier, shards - 1)
+    for part in range(PIECES):
+        first_gather.begin(part)
+    load.wait()
+
+    atoms = d_ref.shape[0]
+
+    def add_squares(step, total):
+        wide = d_ref[:, pl.ds(pl.multiple_of(step * 512, 512), 512)].astype(jnp.float32)
+        wide = wide * wide
+        return total + (
+            (wide[:, :128] + wide[:, 128:256]) + (wide[:, 256:384] + wide[:, 384:])
+        )
+
+    squares = lax.fori_loop(
+        0, width // 512, add_squares, jnp.zeros((atoms, LANES), jnp.float32)
+    )
+    atom_squares = jnp.sum(squares.T, axis=0, keepdims=True)
+    atom_norm = jnp.sqrt(atom_squares + epsilon)
+
+    state = {
+        "corr": jnp.zeros((tokens, atoms), jnp.float32),
+        "energy": jnp.zeros((tokens, LANES), jnp.float32),
+        "grad": jnp.zeros((tokens, atoms), jnp.float32),
+    }
+
+    def correlate(chunk):
+        rows = x_all[chunk]
+        state["corr"] = state["corr"] + lax.dot_general(
+            rows, columns(chunk), (((1,), (1,)), ((), ())), preferred_element_type=jnp.float32
+        )
+        wide = rows.astype(jnp.float32)
+        wide = wide * wide
+        for lane in range(0, piece, LANES):
+            state["energy"] = state["energy"] + wide[:, lane:lane + LANES]
+
+    first_gather.run(correlate)
+    corr = state["corr"]
+    corr_abs = jnp.abs(corr)
+
+    local = jnp.maximum(corr_abs[:, :LANES], corr_abs[:, LANES:])
+    local = jnp.concatenate([local, jnp.zeros((LANES - tokens, LANES), jnp.float32)], axis=0)
+    peaks[0, 0:1, :] = jnp.max(local.T, axis=0, keepdims=True)
+    peaks[0, 1:8, :] = jnp.broadcast_to(
+        jnp.maximum(atom_squares[:, :LANES], atom_squares[:, LANES:]), (7, LANES)
+    )
+
+    def peak_copy(offset):
+        return remote(
+            peaks.at[0], peaks.at[offset], peak_send.at[offset], peak_recv.at[offset],
+            peer_of(offset),
+        )
+
+    def send_peak(offset, carry):
+        peak_copy(offset).start()
+        return carry
+
+    def take_peak(offset, carry):
+        peak_copy(offset).wait_recv()
+        return carry
+
+    lax.fori_loop(1, shards, send_peak, 0)
+    radius = (1.0 / penalty_ratio - 1.0) * jnp.sqrt(
+        jnp.sum(state["energy"], axis=1, keepdims=True) + epsilon
+    )
+    lax.fori_loop(1, shards, take_peak, 0)
+    top = jnp.max(peaks[...], axis=0)
+    peak_value = jnp.broadcast_to(top[0:1, :], (LANES, LANES)).T[:tokens, :] + epsilon
+    widest = jnp.max(top[1:2, :], axis=1, keepdims=True)
+    lipschitz = jnp.broadcast_to(step_scale * (widest + epsilon), (tokens, LANES))
+    threshold = penalty_ratio * peak_value / lipschitz
+    blocks = range(BLK_DEV)
+    keep = [flags_ref[0, block].astype(jnp.float32) for block in blocks]
+    lanes = [slice(block * GROUP_ELEMENTS, (block + 1) * GROUP_ELEMENTS) for block in blocks]
+    first = [
+        keep[block] * shrink(corr[:, lanes[block]] / lipschitz, threshold) for block in blocks
+    ]
+    codes = jnp.concatenate([part.astype(jnp.bfloat16) for part in first], axis=1)
+
+    def share_of(side, offset, part):
+        chunk = (side * ring + chip_at(offset)) * PIECES + part
+        return jnp.dot(codes, columns(chunk), preferred_element_type=jnp.float32)
+
+    order = []
+    for hop in range(right_hops):
+        order.append(right_hops - hop)
+        if hop < left_hops:
+            order.append(hop - left_hops)
+    order.append(0)
+
+    def sib_copy(slot, part):
+        return remote(
+            sib_out.at[slot, part], sib_in.at[slot, part],
+            sib_send.at[slot, part], sib_recv.at[slot, part], to_sibling,
+        )
+
+    def offer(slot):
+        if slot >= ring:
+            return
+        for part in range(PIECES):
+            sib_out[slot, part] = share_of(other, order[slot], part).astype(jnp.bfloat16)
+            made = sib_copy(slot, part)
+            made.start()
+            sent.append(made)
+
+    def chip_sum(slot, part):
+        mine = share_of(core, order[slot], part)
+        sib_copy(slot, part).wait_recv()
+        return mine + sib_in[slot, part].astype(jnp.float32)
+
+    def ring_copy(out, into, row, hop, part, target):
+        return remote(
+            out.at[hop, part], into.at[hop, part],
+            rs_send.at[row + hop, part], rs_recv.at[row + hop, part], target,
+        )
+
+    def pass_on(out, into, row, hop, part, target, slot):
+        total = chip_sum(slot, part)
+        if hop > 0:
+            ring_copy(out, into, row, hop - 1, part, target).wait_recv()
+            total = total + into[hop - 1, part].astype(jnp.float32)
+        out[hop, part] = total.astype(jnp.bfloat16)
+        made = ring_copy(out, into, row, hop, part, target)
+        made.start()
+        sent.append(made)
+
+    early = min(4, ring)
+    for slot in range(early):
+        offer(slot)
+    for hop in range(right_hops):
+        for part in range(PIECES):
+            pass_on(right_out, right_in, 0, hop, part, to_right, order.index(right_hops - hop))
+            if hop < left_hops:
+                pass_on(
+                    left_out, left_in, right_hops, hop, part, to_left,
+                    order.index(hop - left_hops),
+                )
+        offer(early + 2 * hop)
+        offer(early + 2 * hop + 1)
+        if hop == 0:
+            for block in blocks:
+                screen_ref[:, lanes[block]] = (
+                    corr_abs[:, lanes[block]] + radius * atom_norm[:, lanes[block]]
+                ) / peak_value
+
+    second_gather = Gather(r_all, ag2_send, ag2_recv)
+    for part in range(PIECES):
+        total = chip_sum(ring - 1, part)
+        ring_copy(right_out, right_in, 0, right_hops - 1, part, to_right).wait_recv()
+        total = total + right_in[right_hops - 1, part].astype(jnp.float32)
+        ring_copy(left_out, left_in, right_hops, left_hops - 1, part, to_left).wait_recv()
+        total = total + left_in[left_hops - 1, part].astype(jnp.float32)
+        here = slice(part * piece, (part + 1) * piece)
+        residual = total - x_ref[:, here].astype(jnp.float32)
+        resid_ref[:, here] = residual
+        r_all[me * PIECES + part] = residual.astype(jnp.bfloat16)
+        second_gather.begin(part)
+
+    def descend(chunk):
+        state["grad"] = state["grad"] + lax.dot_general(
+            r_all[chunk], columns(chunk), (((1,), (1,)), ((), ())),
+            preferred_element_type=jnp.float32,
+        )
+
+    second_gather.run(descend)
+    for block in blocks:
+        coef_ref[:, lanes[block]] = keep[block] * shrink(
+            first[block] - state["grad"][:, lanes[block]] / lipschitz, threshold
+        )
+
+    for made in sent:
+        made.wait_send()
+
+    def close_peak(offset, carry):
+        peak_copy(offset).wait_send()
+        return carry
+
+    lax.fori_loop(1, shards, close_peak, 0)
+
+
+def on_device(leftover_inputs, codebook_matrix, remaining_tiles):
+    ring, cores = lax.axis_size("inner"), lax.axis_size("outer")
+    tokens, slab = leftover_inputs.shape
+    atoms, width = codebook_matrix.shape
+    wide_enough = slab % (PIECES * LANES) == 0 and width % 512 == 0
+    if not (wide_enough and cores == 2 and ring % 2 == 0 and ring >= 4 and tokens <= LANES):
+        return on_device_narrow(leftover_inputs, codebook_matrix, remaining_tiles)
+    shards = cores * ring
+    piece = slab // PIECES
+    hops = ring - 1
+    step_scale = (1.0 + math.sqrt(atoms * shards / width)) ** 2
+    vmem = pl.BlockSpec(memory_space=pltpu.VMEM)
+    dma = pltpu.SemaphoreType.DMA
+
+    def block(*lead):
+        return pltpu.VMEM((*lead, tokens, piece), jnp.bfloat16)
+
+    return pl.pallas_call(
+        functools.partial(fused_kernel, ring, width, step_scale),
+        out_shape=(
+            jax.ShapeDtypeStruct((tokens, atoms), jnp.float32),
+            jax.ShapeDtypeStruct((tokens, atoms), jnp.float32),
+            jax.ShapeDtypeStruct((tokens, slab), jnp.float32),
+        ),
+        in_specs=[
+            vmem,
+            pl.BlockSpec(memory_space=pl.ANY),
+            pl.BlockSpec(memory_space=pltpu.SMEM),
+        ],
+        out_specs=(vmem, vmem, vmem),
+        scratch_shapes=[
+            pltpu.VMEM((atoms, width), jnp.bfloat16),
+            block(shards * PIECES),
+            block(shards * PIECES),
+            pltpu.VMEM((shards, 8, LANES), jnp.float32),
+            block(ring, PIECES),
+            block(ring, PIECES),
+            block(ring // 2, PIECES),
+            block(ring // 2, PIECES),
+            block(ring // 2 - 1, PIECES),
+            block(ring // 2 - 1, PIECES),
+            dma,
+            dma((hops + ring, PIECES)),
+            dma((hops + ring, PIECES)),
+            dma((hops + ring, PIECES)),
+            dma((hops + ring, PIECES)),
+            dma((shards,)),
+            dma((shards,)),
+            dma((ring, PIECES)),
+            dma((ring, PIECES)),
+            dma((hops, PIECES)),
+            dma((hops, PIECES)),
+        ],
+        compiler_params=pltpu.CompilerParams(
+            collective_id=0, has_side_effects=True, vmem_limit_bytes=40 << 20
+        ),
+    )(leftover_inputs, codebook_matrix, remaining_tiles)
+
+
 def solution(mesh):
     in_specs = (
         P("groups", ("outer", "inner")),

time: 226 us -> 68.1 us (0.30)
  the two profiles are of different devices: /device:TPU:8 before, /device:TPU:0 now
where the time goes in v1:
time: 68.1 us; the launch traced here: 67.8 us
  Pallas kernels  61.4 us (90%)
  local copies, waits for them, and re-layouts  5.73 us (8%)
    pallas_call x1, Pallas kernels, on_device(): pl.pallas_call(functools.partial(fused_kernel, ring, width, step_scale),...  61.4 us
    unnamed x9, local copies, waits for them, and re-layouts  5.73 us

profile of v1, /device:TPU:0, one launch (start us, length us, event | category | flops | bytes accessed | tf_op | source)
XLA Modules:
  0.0 67.8 jit_solution(6414454432779862429)
XLA Ops:
  0.6 0.0 copy-start
  0.6 2.2 %copy-done = bf16[256,8192]{1,0:T(8,128)(2,1)S(1)} copy-done((bf16[256,8192]{1,0:T(8,128)(2,1)S(1)}, bf16[256,8192]{1,0:T(8,128)(2,1)}, u32[]{:S(2)}) %copy-start) | copy-done | bytes 4194328
  2.8 0.0 copy-start.1
  2.8 0.9 %copy-done.1 = bf16[120,512]{1,0:T(8,128)(2,1)S(1)} copy-done((bf16[120,512]{1,0:T(8,128)(2,1)S(1)}, bf16[120,512]{1,0:T(8,128)(2,1)}, u32[]{:S(2)}) %copy-start.1) | copy-done | bytes 122904
  3.7 0.0 copy-start.2
  3.7 0.7 copy-done.2
  4.4 61.4 %shard_map.58 = (f32[120,256]{1,0:T(8,128)S(1)}, f32[120,256]{1,0:T(8,128)S(1)}, f32[120,512]{1,0:T(8,128)S(1)}) custom-call(bf16[120,512]{1,0:T(8,128)(2,1)S(1)} %copy-done.1, bf16[256,8192]{1,0:T(8,128)(2,1)S(1)} %copy-done, s32[1,2]{1,0:T(1,128)S(1)} %copy-done.2), custom_call_target="tpu_custom_call" | custom-call | tf_op jit(solution)/shard_map/pallas_call | solution.py:421
  65.8 0.7 copy.9
  66.4 0.6 copy.10
  67.1 0.7 %copy.11 = f32[120,512]{1,0:T(8,128)} copy(f32[120,512]{1,0:T(8,128)S(1)} %get-tuple-element.8) | data formatting | bytes 491520
Async XLA Ops:
  0.6 2.2 %copy-start = (bf16[256,8192]{1,0:T(8,128)(2,1)S(1)}, bf16[256,8192]{1,0:T(8,128)(2,1)}, u32[]{:S(2)}) copy-start(bf16[256,8192]{1,0:T(8,128)(2,1)} %d_hbm.1) | copy-start | bytes 12582916
  2.8 0.9 %copy-start.1 = (bf16[120,512]{1,0:T(8,128)(2,1)S(1)}, bf16[120,512]{1,0:T(8,128)(2,1)}, u32[]{:S(2)}) copy-start(bf16[120,512]{1,0:T(8,128)(2,1)} %x_ref.1) | copy-start | bytes 368644
  3.7 0.7 copy-start.2

commit v2 on v1

--- a/solution.py
+++ b/solution.py
@@ -100,29 +100,42 @@
     return (screen, coefficients, residual)
 
 
-PIECES = 2
+PIECES = 4
 LANES = 128
 
 
 def fused_kernel(
     ring, width, step_scale,
-    x_ref, d_hbm, flags_ref,
+    x_hbm, d_hbm, flags_hbm,
     screen_ref, coef_ref, resid_ref,
-    d_ref, x_all, r_all, peaks, sib_out, sib_in, right_out, right_in, left_out, left_in,
-    load_sem, ag1_send, ag1_recv, ag2_send, ag2_recv,
+    d_ref, flags_ref, squares, x_all, r_all, peaks, sib_out, sib_in, right_out, right_in, left_out, left_in,
+    load_sem, x_sem, flag_sem, ag1_send, ag1_recv, ag2_send, ag2_recv,
     peak_send, peak_recv, sib_send, sib_recv, rs_send, rs_recv,
 ):
-    tokens, slab = x_ref.shape
+    tokens, slab = x_hbm.shape
     piece = slab // PIECES
     shards = 2 * ring
-    right_hops, left_hops = ring // 2, ring // 2 - 1
+    half_ring = ring // 2
+
+    def goes_right(hop, part):
+        return hop < half_ring - 1 or (hop < half_ring and part < PIECES // 2)
+
+    def goes_left(hop, part):
+        return hop < half_ring - 1 or (hop < half_ring and part >= PIECES // 2)
+
     core = lax.axis_index("outer")
     chip = lax.axis_index("inner")
     me = core * ring + chip
     other = 1 - core
 
-    load = pltpu.make_async_copy(d_hbm, d_ref, load_sem)
-    load.start()
+    x_loads = [
+        pltpu.make_async_copy(
+            x_hbm.at[:, pl.ds(part * piece, piece)], x_all.at[me * PIECES + part], x_sem.at[part]
+        )
+        for part in range(PIECES)
+    ]
+    for made in x_loads:
+        made.start()
 
     barrier = pltpu.get_barrier_semaphore()
 
@@ -130,14 +143,6 @@
         peer = lax.rem(me + offset, shards)
         return {"outer": lax.div(peer, ring), "inner": lax.rem(peer, ring)}
 
-    def greet(offset, carry):
-        pl.semaphore_signal(
-            barrier, inc=1, device_id=peer_of(offset), device_id_type=pl.DeviceIdType.MESH
-        )
-        return carry
-
-    lax.fori_loop(1, shards, greet, 0)
-
     place = jnp.where(lax.rem(chip, 2) == 0, lax.div(chip, 2), ring - 1 - lax.div(chip, 2))
 
     def chip_at(offset):
@@ -147,6 +152,15 @@
     to_right = {"outer": core, "inner": chip_at(1)}
     to_left = {"outer": core, "inner": chip_at(-1)}
     to_sibling = {"outer": other, "inner": chip}
+
+    for target in (to_right, to_left, to_sibling):
+        pl.semaphore_signal(
+            barrier, inc=1, device_id=target, device_id_type=pl.DeviceIdType.MESH
+        )
+    load = pltpu.make_async_copy(d_hbm, d_ref, load_sem)
+    load.start()
+    flag_load = pltpu.make_async_copy(flags_hbm, flags_ref, flag_sem)
+    flag_load.start()
 
     def remote(src, dst, send_sem, recv_sem, target):
         return pltpu.make_async_remote_copy(
@@ -173,74 +187,63 @@
             sent.append(made)
 
         def share(self, slot, part, chunk):
-            self.start(right_hops + left_hops + slot, part, chunk, to_sibling)
+            self.start(2 * half_ring + slot, part, chunk, to_sibling)
 
         def chunk(self, side, offset, part):
             return (side * ring + chip_at(offset)) * PIECES + part
 
         def begin(self, part):
             mine = self.chunk(core, 0, part)
-            self.start(0, part, mine, to_right)
-            self.start(right_hops, part, mine, to_left)
+            if goes_right(0, part):
+                self.start(0, part, mine, to_right)
+            if goes_left(0, part):
+                self.start(half_ring, part, mine, to_left)
             self.share(0, part, mine)
 
         def run(self, consume):
             for part in range(PIECES):
                 consume(self.chunk(core, 0, part))
-            shared = [(0, 0)]
-            for hop in range(right_hops):
+            shared = [(0, 0, part) for part in range(PIECES)]
+            for hop in range(half_ring):
                 fresh = []
                 for part in range(PIECES):
-                    got = self.chunk(core, -1 - hop, part)
-                    self.copy(hop, part, got, to_right).wait_recv()
-                    if hop + 1 < right_hops:
-                        self.start(hop + 1, part, got, to_right)
-                    self.share(1 + 2 * hop, part, got)
-                    if hop < left_hops:
-                        back = self.chunk(core, 1 + hop, part)
-                        self.copy(right_hops + hop, part, back, to_left).wait_recv()
-                        if hop + 1 < left_hops:
-                            self.start(right_hops + hop + 1, part, back, to_left)
-                        self.share(2 + 2 * hop, part, back)
-                        consume(back)
-                    consume(got)
-                fresh.append((1 + 2 * hop, -1 - hop))
-                if hop < left_hops:
-                    fresh.append((2 + 2 * hop, 1 + hop))
+                    landed = []
+                    for goes, row, sign, target in (
+                        (goes_right, 0, -1, to_right), (goes_left, half_ring, 1, to_left)
+                    ):
+                        if not goes(hop, part):
+                            continue
+                        offset = sign * (1 + hop)
+                        got = self.chunk(core, offset, part)
+                        self.copy(row + hop, part, got, target).wait_recv()
+                        if goes(hop + 1, part):
+                            self.start(row + hop + 1, part, got, target)
+                        slot = min(1 + 2 * hop + (sign > 0), ring - 1)
+                        self.share(slot, part, got)
+                        fresh.append((slot, offset, part))
+                        landed.append(got)
+                    for got in landed:
+                        consume(got)
                 self.take(shared, consume)
                 shared = fresh
             self.take(shared, consume)
 
         def take(self, shared, consume):
-            for slot, offset in shared:
-                for part in range(PIECES):
-                    got = self.chunk(other, offset, part)
-                    self.copy(right_hops + left_hops + slot, part, got, to_sibling).wait_recv()
-                    consume(got)
+            for slot, offset, part in shared:
+                got = self.chunk(other, offset, part)
+                self.copy(2 * half_ring + slot, part, got, to_sibling).wait_recv()
+                consume(got)
 
     first_gather = Gather(x_all, ag1_send, ag1_recv)
+    pl.semaphore_wait(barrier, 3)
     for part in range(PIECES):
-        x_all[me * PIECES + part] = x_ref[:, part * piece:(part + 1) * piece]
-    pl.semaphore_wait(barrier, shards - 1)
-    for part in range(PIECES):
+        x_loads[part].wait()
         first_gather.begin(part)
+    squares[...] = jnp.zeros_like(squares)
+    flag_load.wait()
     load.wait()
 
     atoms = d_ref.shape[0]
-
-    def add_squares(step, total):
-        wide = d_ref[:, pl.ds(pl.multiple_of(step * 512, 512), 512)].astype(jnp.float32)
-        wide = wide * wide
-        return total + (
-            (wide[:, :128] + wide[:, 128:256]) + (wide[:, 256:384] + wide[:, 384:])
-        )
-
-    squares = lax.fori_loop(
-        0, width // 512, add_squares, jnp.zeros((atoms, LANES), jnp.float32)
-    )
-    atom_squares = jnp.sum(squares.T, axis=0, keepdims=True)
-    atom_norm = jnp.sqrt(atom_squares + epsilon)
-
     state = {
         "corr": jnp.zeros((tokens, atoms), jnp.float32),
         "energy": jnp.zeros((tokens, LANES), jnp.float32),
@@ -248,10 +251,13 @@
     }
 
     def correlate(chunk):
-        rows = x_all[chunk]
+        rows, held = x_all[chunk], columns(chunk)
         state["corr"] = state["corr"] + lax.dot_general(
-            rows, columns(chunk), (((1,), (1,)), ((), ())), preferred_element_type=jnp.float32
-        )
+            rows, held, (((1,), (1,)), ((), ())), preferred_element_type=jnp.float32
+        )
+        broad = held.astype(jnp.float32)
+        broad = broad * broad
+        squares[...] += sum(broad[:, lane:lane + LANES] for lane in range(0, piece, LANES))
         wide = rows.astype(jnp.float32)
         wide = wide * wide
         for lane in range(0, piece, LANES):
@@ -260,6 +266,8 @@
     first_gather.run(correlate)
     corr = state["corr"]
     corr_abs = jnp.abs(corr)
+    atom_squares = jnp.sum(squares[...].T, axis=0, keepdims=True)
+    atom_norm = jnp.sqrt(atom_squares + epsilon)
 
     local = jnp.maximum(corr_abs[:, :LANES], corr_abs[:, LANES:])
     local = jnp.concatenate([local, jnp.zeros((LANES - tokens, LANES), jnp.float32)], axis=0)
@@ -304,11 +312,9 @@
         chunk = (side * ring + chip_at(offset)) * PIECES + part
         return jnp.dot(codes, columns(chunk), preferred_element_type=jnp.float32)
 
-    order = []
-    for hop in range(right_hops):
-        order.append(right_hops - hop)
-        if hop < left_hops:
-            order.append(hop - left_hops)
+    order = [half_ring]
+    for away in range(half_ring - 1, 0, -1):
+        order += [away, -away]
     order.append(0)
 
     def sib_copy(slot, part):
@@ -337,9 +343,23 @@
             rs_send.at[row + hop, part], rs_recv.at[row + hop, part], target,
         )
 
-    def pass_on(out, into, row, hop, part, target, slot):
+    ways = (
+        (goes_right, right_out, right_in, 0, 1, to_right),
+        (goes_left, left_out, left_in, half_ring, -1, to_left),
+    )
+
+    def starts_at(goes, part):
+        return 0 if goes(half_ring - 1, part) else 1
+
+    def pass_on(way, hop, part):
+        goes, out, into, row, sign, target = way
+        first_hop = starts_at(goes, part)
+        if hop < first_hop:
+            return
+        away = half_ring - hop
+        slot = order.index(away if away == half_ring else sign * away)
         total = chip_sum(slot, part)
-        if hop > 0:
+        if hop > first_hop:
             ring_copy(out, into, row, hop - 1, part, target).wait_recv()
             total = total + into[hop - 1, part].astype(jnp.float32)
         out[hop, part] = total.astype(jnp.bfloat16)
@@ -347,17 +367,13 @@
         made.start()
         sent.append(made)
 
-    early = min(4, ring)
+    early = min(3, ring)
     for slot in range(early):
         offer(slot)
-    for hop in range(right_hops):
+    for hop in range(half_ring):
         for part in range(PIECES):
-            pass_on(right_out, right_in, 0, hop, part, to_right, order.index(right_hops - hop))
-            if hop < left_hops:
-                pass_on(
-                    left_out, left_in, right_hops, hop, part, to_left,
-                    order.index(hop - left_hops),
-                )
+            for way in ways:
+                pass_on(way, hop, part)
         offer(early + 2 * hop)
         offer(early + 2 * hop + 1)
         if hop == 0:
@@ -369,12 +385,11 @@
     second_gather = Gather(r_all, ag2_send, ag2_recv)
     for part in range(PIECES):
         total = chip_sum(ring - 1, part)
-        ring_copy(right_out, right_in, 0, right_hops - 1, part, to_right).wait_recv()
-        total = total + right_in[right_hops - 1, part].astype(jnp.float32)
-        ring_copy(left_out, left_in, right_hops, left_hops - 1, part, to_left).wait_recv()
-        total = total + left_in[left_hops - 1, part].astype(jnp.float32)
+        for goes, out, into, row, sign, target in ways:
+            ring_copy(out, into, row, half_ring - 1, part, target).wait_recv()
+            total = total + into[half_ring - 1, part].astype(jnp.float32)
         here = slice(part * piece, (part + 1) * piece)
-        residual = total - x_ref[:, here].astype(jnp.float32)
+        residual = total - x_all[me * PIECES + part].astype(jnp.float32)
         resid_ref[:, here] = residual
         r_all[me * PIECES + part] = residual.astype(jnp.bfloat16)
         second_gather.begin(part)
@@ -410,7 +425,7 @@
         return on_device_narrow(leftover_inputs, codebook_matrix, remaining_tiles)
     shards = cores * ring
     piece = slab // PIECES
-    hops = ring - 1
+    hops = ring
     step_scale = (1.0 + math.sqrt(atoms * shards / width)) ** 2
     vmem = pl.BlockSpec(memory_space=pltpu.VMEM)
     dma = pltpu.SemaphoreType.DMA
@@ -426,13 +441,15 @@
             jax.ShapeDtypeStruct((tokens, slab), jnp.float32),
         ),
         in_specs=[
-            vmem,
             pl.BlockSpec(memory_space=pl.ANY),
-            pl.BlockSpec(memory_space=pltpu.SMEM),
+            pl.BlockSpec(memory_space=pl.ANY),
+            pl.BlockSpec(memory_space=pl.ANY),
         ],
         out_specs=(vmem, vmem, vmem),
         scratch_shapes=[
             pltpu.VMEM((atoms, width), jnp.bfloat16),
+            pltpu.SMEM((1, BLK_DEV), jnp.int32),
+            pltpu.VMEM((atoms, LANES), jnp.float32),
             block(shards * PIECES),
             block(shards * PIECES),
             pltpu.VMEM((shards, 8, LANES), jnp.float32),
@@ -440,8 +457,10 @@
             block(ring, PIECES),
             block(ring // 2, PIECES),
             block(ring // 2, PIECES),
-            block(ring // 2 - 1, PIECES),
-            block(ring // 2 - 1, PIECES),
+            block(ring // 2, PIECES),
+            block(ring // 2, PIECES),
+            dma,
+            dma((PIECES,)),
             dma,
             dma((hops + ring, PIECES)),
             dma((hops + ring, PIECES)),

time: 68.1 us -> 64.3 us (0.944)
  Pallas kernels: 61.4 us -> 57.7 us
    pallas_call x1, Pallas kernels: 61.4 us -> 57.7 us  [on_device(): pl.pallas_call(functools.partial(fused_kernel, ring, width, step_scale),...]
where the time goes in v2:
time: 64.3 us; the launch traced here: 64.1 us
  Pallas kernels  57.7 us (90%)
  local copies, waits for them, and re-layouts  5.73 us (9%)
  between operations  0.65 us (1%)
    pallas_call x1, Pallas kernels, on_device(): pl.pallas_call(functools.partial(fused_kernel, ring, width, step_scale),...  57.7 us
    unnamed x9, local copies, waits for them, and re-layouts  5.73 us

profile of v2, /device:TPU:0, one launch (start us, length us, event | category | flops | bytes accessed | tf_op | source)
XLA Modules:
  0.0 64.1 jit_solution(12120327283140596115)
XLA Ops:
  0.6 0.0 copy-start
  0.6 2.2 %copy-done = bf16[256,8192]{1,0:T(8,128)(2,1)S(1)} copy-done((bf16[256,8192]{1,0:T(8,128)(2,1)S(1)}, bf16[256,8192]{1,0:T(8,128)(2,1)}, u32[]{:S(2)}) %copy-start) | copy-done | bytes 4194328
  2.8 0.0 copy-start.1
  2.8 0.9 %copy-done.1 = bf16[120,512]{1,0:T(8,128)(2,1)S(1)} copy-done((bf16[120,512]{1,0:T(8,128)(2,1)S(1)}, bf16[120,512]{1,0:T(8,128)(2,1)}, u32[]{:S(2)}) %copy-start.1) | copy-done | bytes 122904
  3.7 0.0 copy-start.2
  3.7 0.7 %copy-done.2 = s32[1,2]{1,0:T(1,128)S(1)} copy-done((s32[1,2]{1,0:T(1,128)S(1)}, s32[1,2]{1,0:T(1,128)}, u32[]{:S(2)}) %copy-start.2) | copy-done | bytes 32
  4.4 57.7 %shard_map.58 = (f32[120,256]{1,0:T(8,128)S(1)}, f32[120,256]{1,0:T(8,128)S(1)}, f32[120,512]{1,0:T(8,128)S(1)}) custom-call(bf16[120,512]{1,0:T(8,128)(2,1)S(1)} %copy-done.1, bf16[256,8192]{1,0:T(8,128)(2,1)S(1)} %copy-done, s32[1,2]{1,0:T(1,128)S(1)} %copy-done.2), custom_call_target="tpu_custom_call" | custom-call | tf_op jit(solution)/shard_map/pallas_call | solution.py:436
  62.1 0.7 %copy.9 = f32[120,256]{1,0:T(8,128)} copy(f32[120,256]{1,0:T(8,128)S(1)} %get-tuple-element.6) | data formatting | bytes 245760
  62.7 0.6 %copy.10 = f32[120,256]{1,0:T(8,128)} copy(f32[120,256]{1,0:T(8,128)S(1)} %get-tuple-element.7) | data formatting | bytes 245760
  63.4 0.7 %copy.11 = f32[120,512]{1,0:T(8,128)} copy(f32[120,512]{1,0:T(8,128)S(1)} %get-tuple-element.8) | data formatting | bytes 491520
Async XLA Ops:
  0.6 2.2 %copy-start = (bf16[256,8192]{1,0:T(8,128)(2,1)S(1)}, bf16[256,8192]{1,0:T(8,128)(2,1)}, u32[]{:S(2)}) copy-start(bf16[256,8192]{1,0:T(8,128)(2,1)} %d_hbm.1) | copy-start | bytes 12582916
  2.8 0.9 %copy-start.1 = (bf16[120,512]{1,0:T(8,128)(2,1)S(1)}, bf16[120,512]{1,0:T(8,128)(2,1)}, u32[]{:S(2)}) copy-start(bf16[120,512]{1,0:T(8,128)(2,1)} %x_hbm.1) | copy-start | bytes 368644
  3.7 0.7 %copy-start.2 = (s32[1,2]{1,0:T(1,128)S(1)}, s32[1,2]{1,0:T(1,128)}, u32[]{:S(2)}) copy-start(s32[1,2]{1,0:T(1,128)} %flags_hbm.1) | copy-start | bytes 28

commit v3 on v2

--- a/solution.py
+++ b/solution.py
@@ -198,9 +198,10 @@
                 self.start(0, part, mine, to_right)
             if goes_left(0, part):
                 self.start(half_ring, part, mine, to_left)
-            self.share(0, part, mine)
 
         def run(self, consume):
+            for part in range(PIECES):
+                self.share(0, part, self.chunk(core, 0, part))
             for part in range(PIECES):
                 consume(self.chunk(core, 0, part))
             shared = [(0, 0, part) for part in range(PIECES)]
@@ -376,11 +377,6 @@
                 pass_on(way, hop, part)
         offer(early + 2 * hop)
         offer(early + 2 * hop + 1)
-        if hop == 0:
-            for block in blocks:
-                screen_ref[:, lanes[block]] = (
-                    corr_abs[:, lanes[block]] + radius * atom_norm[:, lanes[block]]
-                ) / peak_value
 
     second_gather = Gather(r_all, ag2_send, ag2_recv)
     for part in range(PIECES):
@@ -400,6 +396,10 @@
             preferred_element_type=jnp.float32,
         )
 
+    for block in blocks:
+        screen_ref[:, lanes[block]] = (
+            corr_abs[:, lanes[block]] + radius * atom_norm[:, lanes[block]]
+        ) / peak_value
     second_gather.run(descend)
     for block in blocks:
         coef_ref[:, lanes[block]] = keep[block] * shrink(

time: 64.3 us -> 64.4 us (level)
  no operation moved by 1% of the time
where the time goes in v3:
time: 64.4 us; the launch traced here: 64.2 us
  Pallas kernels  57.8 us (90%)
  local copies, waits for them, and re-layouts  5.73 us (9%)
  between operations  0.65 us (1%)
    pallas_call x1, Pallas kernels, on_device(): pl.pallas_call(functools.partial(fused_kernel, ring, width, step_scale),...  57.8 us
    unnamed x9, local copies, waits for them, and re-layouts  5.73 us

profile of v3, /device:TPU:0, one launch (start us, length us, event | category | flops | bytes accessed | tf_op | source)
XLA Modules:
  0.0 64.2 jit_solution(10735681872502033128)
XLA Ops:
  0.6 0.0 copy-start
  0.6 2.2 %copy-done = bf16[256,8192]{1,0:T(8,128)(2,1)S(1)} copy-done((bf16[256,8192]{1,0:T(8,128)(2,1)S(1)}, bf16[256,8192]{1,0:T(8,128)(2,1)}, u32[]{:S(2)}) %copy-start) | copy-done | bytes 4194328
  2.8 0.0 copy-start.1
  2.8 0.9 %copy-done.1 = bf16[120,512]{1,0:T(8,128)(2,1)S(1)} copy-done((bf16[120,512]{1,0:T(8,128)(2,1)S(1)}, bf16[120,512]{1,0:T(8,128)(2,1)}, u32[]{:S(2)}) %copy-start.1) | copy-done | bytes 122904
  3.7 0.0 copy-start.2
  3.7 0.7 %copy-done.2 = s32[1,2]{1,0:T(1,128)S(1)} copy-done((s32[1,2]{1,0:T(1,128)S(1)}, s32[1,2]{1,0:T(1,128)}, u32[]{:S(2)}) %copy-start.2) | copy-done | bytes 32
  4.4 57.8 %shard_map.58 = (f32[120,256]{1,0:T(8,128)S(1)}, f32[120,256]{1,0:T(8,128)S(1)}, f32[120,512]{1,0:T(8,128)S(1)}) custom-call(bf16[120,512]{1,0:T(8,128)(2,1)S(1)} %copy-done.1, bf16[256,8192]{1,0:T(8,128)(2,1)S(1)} %copy-done, s32[1,2]{1,0:T(1,128)S(1)} %copy-done.2), custom_call_target="tpu_custom_call" | custom-call | tf_op jit(solution)/shard_map/pallas_call | solution.py:436
  62.2 0.7 %copy.9 = f32[120,256]{1,0:T(8,128)} copy(f32[120,256]{1,0:T(8,128)S(1)} %get-tuple-element.6) | data formatting | bytes 245760
  62.9 0.6 %copy.10 = f32[120,256]{1,0:T(8,128)} copy(f32[120,256]{1,0:T(8,128)S(1)} %get-tuple-element.7) | data formatting | bytes 245760
  63.5 0.7 %copy.11 = f32[120,512]{1,0:T(8,128)} copy(f32[120,512]{1,0:T(8,128)S(1)} %get-tuple-element.8) | data formatting | bytes 491520
Async XLA Ops:
  0.6 2.2 %copy-start = (bf16[256,8192]{1,0:T(8,128)(2,1)S(1)}, bf16[256,8192]{1,0:T(8,128)(2,1)}, u32[]{:S(2)}) copy-start(bf16[256,8192]{1,0:T(8,128)(2,1)} %d_hbm.1) | copy-start | bytes 12582916
  2.8 0.9 %copy-start.1 = (bf16[120,512]{1,0:T(8,128)(2,1)S(1)}, bf16[120,512]{1,0:T(8,128)(2,1)}, u32[]{:S(2)}) copy-start(bf16[120,512]{1,0:T(8,128)(2,1)} %x_hbm.1) | copy-start | bytes 368644
  3.7 0.7 %copy-start.2 = (s32[1,2]{1,0:T(1,128)S(1)}, s32[1,2]{1,0:T(1,128)}, u32[]{:S(2)}) copy-start(s32[1,2]{1,0:T(1,128)} %flags_hbm.1) | copy-start | bytes 28
